TPU v7x, 32 devices: a whole 2x2x4 slice. The times are simulated.
32 devices in a mesh: gx: 8 (over z, y), gy: 2 (over core), gz: 2 (over x).
Axes of the slice: x: 2, y: 2, z: 4, core: 2. Of those that a mesh axis runs over, the one named last changes fastest.
Arguments:
- conserved: bfloat16 [5, 64, 16, 256], P(None, 'gx', 'gy', 'gz'), may hold values from -0.5 to 5, as said below
- sigma_prev: float32 [64, 16, 256], P('gx', 'gy', 'gz'), may hold values from -6 to 6
Outputs:
- new_state: float32 [5, 64, 16, 256], P(None, 'gx', 'gy', 'gz')
- entropic: float32 [64, 16, 256], P('gx', 'gy', 'gz')
Inputs may be any that keep to these rules, and one draw needn't show every extreme that they name: `conserved`: field 0 (density) lies in 0.5 to 2, fields 1 to 3 (momenta) in -0.5 to 0.5, field 4 (total energy) in 2 to 5.
All inputs are finite; a program needn't handle non-finite values.
Results may differ from a plain program's by a relative error of at most 0.0013.
Values may be sent and summed in bfloat16 or wider, within the bound.
A program may use at most 64 MiB of HBM per device.

v0:
```python
import jax
import jax.numpy as jnp
from jax import lax
from jax.sharding import PartitionSpec as P

SWEEPS = 4


gamma_gas = 1.4
alpha_reg = 4.0
time_step = 0.08


def extended(cells, sides, width):
    for axis, dim in sides:
        count = lax.axis_size(axis)
        head = lax.slice_in_dim(cells, 0, width, axis=dim)
        tail = lax.slice_in_dim(cells, cells.shape[dim] - width, cells.shape[dim], axis=dim)
        cells = jnp.concatenate(
            [
                lax.ppermute(tail, axis, [(i, (i + 1) % count) for i in range(count)]),
                cells,
                lax.ppermute(head, axis, [((i + 1) % count, i) for i in range(count)]),
            ],
            axis=dim,
        )
    return cells


def crop(tensor, margin):
    return tensor[
        ...,
        margin : tensor.shape[-3] - margin,
        margin : tensor.shape[-2] - margin,
        margin : tensor.shape[-1] - margin,
    ]


def cut_axis(tensor, axis_dim, start, length):
    return lax.slice_in_dim(tensor, start, start + length, axis=axis_dim)


def trim_except(tensor, keep_axis, margin):
    for spatial in range(3):
        if spatial != keep_axis:
            axis_dim = tensor.ndim - 3 + spatial
            tensor = cut_axis(tensor, axis_dim, margin, tensor.shape[axis_dim] - 2 * margin)
    return tensor


def central(tensor, spatial):
    axis_dim = tensor.ndim - 3 + spatial
    length = tensor.shape[axis_dim] - 2
    return 0.5 * (cut_axis(tensor, axis_dim, 2, length) - cut_axis(tensor, axis_dim, 0, length))


def stencil(padded):
    center = padded[1:-1, 1:-1, 1:-1]
    beside_all = [
        padded[2:, 1:-1, 1:-1],
        padded[:-2, 1:-1, 1:-1],
        padded[1:-1, 2:, 1:-1],
        padded[1:-1, :-2, 1:-1],
        padded[1:-1, 1:-1, 2:],
        padded[1:-1, 1:-1, :-2],
    ]
    return (center, beside_all)


def sweep(sigma_pad, inverse_pad, source):
    sigma_mid, sigma_around = stencil(sigma_pad)
    inverse_mid, inverse_around = stencil(inverse_pad)
    numerator = source
    denominator = inverse_mid
    for neighbor_sigma, neighbor_inverse in zip(sigma_around, inverse_around):
        weight = alpha_reg * 0.5 * (inverse_mid + neighbor_inverse)
        numerator = numerator + weight * neighbor_sigma
        denominator = denominator + weight
    return numerator / denominator


def entropic_source(halo_state, cut_cells):
    region = crop(halo_state, cut_cells)
    velocity = region[1:4] / region[0]
    gradient = [trim_except(central(velocity, spatial), spatial, 1) for spatial in range(3)]
    divergence = gradient[0][0] + gradient[1][1] + gradient[2][2]
    product = divergence * divergence
    for first in range(3):
        for second in range(3):
            product = product + gradient[first][second] * gradient[second][first]
    return alpha_reg * product


def physical_flux(values, spatial):
    density = values[0]
    velocity = values[1:4] / density
    kinetic = 0.5 * (values[1] * velocity[0] + values[2] * velocity[1] + values[3] * velocity[2])
    pressure = (gamma_gas - 1.0) * (values[4] - kinetic)
    normal = velocity[spatial]
    momentum = [values[1 + component] * normal for component in range(3)]
    momentum[spatial] = momentum[spatial] + pressure
    flux_vec = jnp.stack([values[1 + spatial]] + momentum + [(values[4] + pressure) * normal])
    wave_speed = jnp.abs(normal) + jnp.sqrt(gamma_gas * jnp.abs(pressure) / density)
    return (flux_vec, wave_speed)


def flux_divergence(halo_state, sigma_pad):
    summed = None
    for spatial in range(3):
        pencil = trim_except(halo_state, spatial, 3)
        axis_dim = spatial + 1
        face_count = pencil.shape[axis_dim] - 5
        shifted = [cut_axis(pencil, axis_dim, offset, face_count) for offset in range(6)]
        left_state = (
            2.0 * shifted[0]
            - 13.0 * shifted[1]
            + 47.0 * shifted[2]
            + 27.0 * shifted[3]
            - 3.0 * shifted[4]
        ) / 60.0
        right_state = (
            2.0 * shifted[5]
            - 13.0 * shifted[4]
            + 47.0 * shifted[3]
            + 27.0 * shifted[2]
            - 3.0 * shifted[1]
        ) / 60.0
        flux_left, speed_left = physical_flux(left_state, spatial)
        flux_right, speed_right = physical_flux(right_state, spatial)
        numeric = 0.5 * (flux_left + flux_right) - 0.5 * jnp.maximum(speed_left, speed_right) * (
            right_state - left_state
        )
        change = cut_axis(numeric, axis_dim, 1, face_count - 1) - cut_axis(
            numeric, axis_dim, 0, face_count - 1
        )
        sigma_line = trim_except(sigma_pad, spatial, 1)
        grad_sigma = central(sigma_line, spatial)
        vel_line = cut_axis(pencil, axis_dim, 2, face_count + 1)
        vel_normal = vel_line[1 + spatial] / vel_line[0]
        power_term = central(sigma_line * vel_normal, spatial)
        update = [change[index] for index in range(5)]
        update[1 + spatial] = update[1 + spatial] + grad_sigma
        update[4] = update[4] + power_term
        increment = jnp.stack(update)
        summed = increment if summed is None else summed + increment
    return -summed


def per_device(conserved, sigma_prev):
    initial = conserved.astype(jnp.float32)
    section_state = conserved
    entropic = sigma_prev
    new_state = initial
    for section_index in range(2):
        depth_wide = SWEEPS + 1
        halo_wide = extended(section_state, (("gx", 1), ("gy", 2), ("gz", 3)), depth_wide).astype(
            jnp.float32
        )
        sigma_pad = extended(entropic, (("gx", 0), ("gy", 1), ("gz", 2)), depth_wide)
        source_wide = entropic_source(halo_wide, 0)
        inverse_wide = 1.0 / halo_wide[0]
        for sweep_index in range(SWEEPS):
            sigma_pad = sweep(
                sigma_pad, crop(inverse_wide, sweep_index), crop(source_wide, sweep_index)
            )
        entropic = crop(sigma_pad, 1)
        tendency = flux_divergence(crop(halo_wide, depth_wide - 3), sigma_pad)
        if section_index == 0:
            section_state = (initial + time_step * tendency).astype(jnp.bfloat16)
        else:
            new_state = 0.5 * (initial + section_state.astype(jnp.float32) + time_step * tendency)
    return (new_state, entropic)


def solution(mesh):
    in_specs = (P(None, "gx", "gy", "gz"), P("gx", "gy", "gz"))
    out_specs = (P(None, "gx", "gy", "gz"), P("gx", "gy", "gz"))
    return jax.shard_map(
        per_device, mesh=mesh, in_specs=in_specs, out_specs=out_specs, check_vma=False
    )
```

profile of v0, /device:TPU:0, one launch (start us, length us, event | category | flops | bytes accessed | tf_op | source)
XLA Modules:
  0.0 109.3 jit_solution(14720838350901610903)
XLA Ops:
  1.4 3.0 %collective-permute-start.6 = (f32[5,8,128]{2,1,0:T(8,128)S(1)}, f32[5,8,128]{2,1,0:T(8,128)S(1)}, u32[]{:S(2)}, u32[]{:S(2)}) collective-permute-start(f32[5,8,128]{2,1,0:T(8,128)S(1)} %get-tuple-element.99), channel_id=1, source_target_pairs={{0,4},{4,8},{8,12},{12,16},{16,20},{20,24},{24,28},{28,0},{1,5},{5... | collective-permute-start | bytes 61448 | tf_op jit(solution)/shard_map/ppermute | solution.py:21
  5.3 1.6 %collective-permute-start = (bf16[5,5,8,128]{3,2,1,0:T(8,128)(2,1)S(1)}, bf16[5,5,8,128]{3,2,1,0:T(8,128)(2,1)S(1)}, u32[]{:S(2)}, u32[]{:S(2)}) collective-permute-start(bf16[5,5,8,128]{3,2,1,0:T(8,128)(2,1)S(1)} %get-tuple-element.93), channel_id=1, source_target_pairs={{0,4},{4,8},{8,12},{12,16},{16,20},{20,24},{24,28},{28,0},{1,5},{5... | collective-permute-start | bytes 153608 | tf_op jit(solution)/shard_map/ppermute | solution.py:21
  6.9 3.2 %collective-permute-start.1 = (bf16[5,5,8,128]{3,2,1,0:T(8,128)(2,1)S(1)}, bf16[5,5,8,128]{3,2,1,0:T(8,128)(2,1)S(1)}, u32[]{:S(2)}, u32[]{:S(2)}) collective-permute-start(bf16[5,5,8,128]{3,2,1,0:T(8,128)(2,1)S(1)} %get-tuple-element.92), channel_id=1, source_target_pairs={{4,0},{8,4},{12,8},{16,12},{20,16},{24,20},{28,24},{0,28},{5,1},{9... | collective-permute-start | bytes 153608 | tf_op jit(solution)/shard_map/ppermute | solution.py:23
  11.3 2.6 %collective-permute-done.7 = f32[5,8,128]{2,1,0:T(8,128)S(1)} collective-permute-done((f32[5,8,128]{2,1,0:T(8,128)S(1)}, f32[5,8,128]{2,1,0:T(8,128)S(1)}, u32[]{:S(2)}, u32[]{:S(2)}) %collective-permute-start.7) | collective-permute-done | bytes 20512 | tf_op jit(solution)/shard_map/ppermute | solution.py:23
  15.6 3.4 %copy.68 = bf16[5,18,8,128]{2,1,3,0:T(8,128)(2,1)} copy(bf16[5,18,8,128]{3,2,1,0:T(8,128)(2,1)S(1)} %constant_dynamic-update-slice_fusion) | data formatting | bytes 368640 | tf_op jit(solution)/shard_map/concatenate | solution.py:19
  20.0 1.6 %collective-permute-start.10 = (f32[18,18,5]{2,1,0:T(8,128)S(1)}, f32[18,18,5]{2,1,0:T(8,128)S(1)}, u32[]{:S(2)}, u32[]{:S(2)}) collective-permute-start(f32[18,18,5]{2,1,0:T(8,128)S(1)} %get-tuple-element.64), channel_id=1, source_target_pairs={{0,1},{1,0},{2,3},{3,2},{4,5},{5,4},{6,7},{7,6},{8,9},{9,8},{10,11... | collective-permute-start | bytes 19448 | tf_op jit(solution)/shard_map/ppermute | solution.py:21
  22.1 3.6 %copy.67 = bf16[5,18,5,128]{2,1,3,0:T(8,128)(2,1)} copy(bf16[5,18,5,128]{3,1,2,0:T(8,128)(2,1)S(1)} %collective-permute-done.2) | data formatting | bytes 230400 | tf_op jit(solution)/shard_map/ppermute | solution.py:21
  25.6 3.6 %copy.69 = bf16[5,18,5,128]{2,1,3,0:T(8,128)(2,1)} copy(bf16[5,18,5,128]{3,1,2,0:T(8,128)(2,1)S(1)} %collective-permute-done.3) | data formatting | bytes 230400 | tf_op jit(solution)/shard_map/ppermute | solution.py:23
  29.2 6.6 %pad_maximum_fusion = bf16[5,18,18,128]{2,1,3,0:T(8,128)(2,1)S(1)} fusion(bf16[5,18,5,128]{2,1,3,0:T(8,128)(2,1)} %copy.69, bf16[5,18,8,128]{2,1,3,0:T(8,128)(2,1)} %copy.68, bf16[5,18,5,128]{2,1,3,0:T(8,128)(2,1)} %copy.67), kind=kLoop, calls=%fused_computation | loop fusion | flops 1244160 | bytes 829440 | tf_op jit(solution)/shard_map/concatenate | solution.py:19
  35.8 1.9 %copy-done.1 = bf16[5,18,18,128]{2,1,3,0:T(8,128)(2,1)} copy-done((bf16[5,18,18,128]{2,1,3,0:T(8,128)(2,1)}, bf16[5,18,18,128]{2,1,3,0:T(8,128)(2,1)S(1)}, u32[]{:S(2)}) %copy-start.1) | copy-done | bytes 414744
  37.7 1.6 %collective-permute-start.4 = (bf16[5,18,18,5]{2,1,3,0:T(8,128)(2,1)S(1)}, bf16[5,18,18,5]{2,1,3,0:T(8,128)(2,1)S(1)}, u32[]{:S(2)}, u32[]{:S(2)}) collective-permute-start(bf16[5,18,18,5]{2,1,3,0:T(8,128)(2,1)S(1)} %get-tuple-element.28), channel_id=1, source_target_pairs={{0,1},{1,0},{2,3},{3,2},{4,5},{5,4},{6,7},{7,6},{8,9},{9,8},{10,11... | collective-permute-start | bytes 48608 | tf_op jit(solution)/shard_map/ppermute | solution.py:21
  40.1 4.6 %copy.71 = bf16[5,18,18,128]{3,2,1,0:T(8,128)(2,1)S(1)} copy(bf16[5,18,18,128]{2,1,3,0:T(8,128)(2,1)} %copy-done.1) | data formatting | bytes 829440 | tf_op jit(solution)/shard_map/concatenate | solution.py:19
  49.0 1.3 %fusion.63 = (f32[16,16,136]{2,1,0:T(8,128)S(1)}, f32[16,16,136]{2,1,0:T(8,128)S(1)}) fusion(f32[18,18,138]{2,1,0:T(8,128)S(1)} %pad_maximum_fusion.2, f32[18,18,138]{2,1,0:T(8,128)S(1)} %broadcast_divide_fusion.1, f32[3,18,18,136]{3,2,1,0:T(8,128)S(1)} %fusion.1, f32[3,18,16,138]{3,2,1,0:T(8,128)S(1)} %fusion.5, f32[3,16,18,138]{3,2,1,0:T(8,128)S(1)} %fusion.3), kind=kLoop, calls=%fused_computation.107 | loop fusion | flops 1740800 | bytes 3342336 | tf_op jit(solution)/shard_map/div | solution.py:79
  55.8 4.7 %collective-permute-start.19 = (f32[5,8,128]{2,1,0:T(8,128)S(1)}, f32[5,8,128]{2,1,0:T(8,128)S(1)}, u32[]{:S(2)}, u32[]{:S(2)}) collective-permute-start(f32[5,8,128]{2,1,0:T(8,128)S(1)} %get-tuple-element.89), channel_id=1, source_target_pairs={{4,0},{8,4},{12,8},{16,12},{20,16},{24,20},{28,24},{0,28},{5,1},{9... | collective-permute-start | bytes 61448 | tf_op jit(solution)/shard_map/ppermute | solution.py:23
  60.8 4.7 %collective-permute-start.13 = (bf16[5,5,8,128]{3,2,1,0:T(8,128)(2,1)S(1)}, bf16[5,5,8,128]{3,2,1,0:T(8,128)(2,1)S(1)}, u32[]{:S(2)}, u32[]{:S(2)}) collective-permute-start(bf16[5,5,8,128]{3,2,1,0:T(8,128)(2,1)S(1)} %get-tuple-element.91), channel_id=1, source_target_pairs={{4,0},{8,4},{12,8},{16,12},{20,16},{24,20},{28,24},{0,28},{5,1},{9... | collective-permute-start | bytes 153608 | tf_op jit(solution)/shard_map/ppermute | solution.py:23
  66.2 1.4 %collective-permute-done.12 = bf16[5,5,8,128]{3,2,1,0:T(8,128)(2,1)S(1)} collective-permute-done((bf16[5,5,8,128]{3,2,1,0:T(8,128)(2,1)S(1)}, bf16[5,5,8,128]{3,2,1,0:T(8,128)(2,1)S(1)}, u32[]{:S(2)}, u32[]{:S(2)}) %collective-permute-start.12) | collective-permute-done | bytes 51232 | tf_op jit(solution)/shard_map/ppermute | solution.py:21
  67.7 3.7 %copy.80 = bf16[5,18,8,128]{2,1,3,0:T(8,128)(2,1)} copy(bf16[5,18,8,128]{3,2,1,0:T(8,128)(2,1)S(1)} %pad_maximum_fusion.6) | data formatting | bytes 368640 | tf_op jit(solution)/shard_map/concatenate | solution.py:19
  72.3 1.6 %collective-permute-start.22 = (f32[18,18,5]{2,1,0:T(8,128)S(1)}, f32[18,18,5]{2,1,0:T(8,128)S(1)}, u32[]{:S(2)}, u32[]{:S(2)}) collective-permute-start(f32[18,18,5]{2,1,0:T(8,128)S(1)} %get-tuple-element.62), channel_id=1, source_target_pairs={{0,1},{1,0},{2,3},{3,2},{4,5},{5,4},{6,7},{7,6},{8,9},{9,8},{10,11... | collective-permute-start | bytes 19448 | tf_op jit(solution)/shard_map/ppermute | solution.py:21
  74.4 3.6 %copy.79 = bf16[5,18,5,128]{2,1,3,0:T(8,128)(2,1)} copy(bf16[5,18,5,128]{3,1,2,0:T(8,128)(2,1)S(1)} %collective-permute-done.14) | data formatting | bytes 230400 | tf_op jit(solution)/shard_map/ppermute | solution.py:21
  78.0 3.6 %copy.81 = bf16[5,18,5,128]{2,1,3,0:T(8,128)(2,1)} copy(bf16[5,18,5,128]{3,1,2,0:T(8,128)(2,1)S(1)} %collective-permute-done.15) | data formatting | bytes 230400 | tf_op jit(solution)/shard_map/ppermute | solution.py:23
  81.5 6.6 %pad_maximum_fusion.1 = bf16[5,18,18,128]{2,1,3,0:T(8,128)(2,1)S(1)} fusion(bf16[5,18,5,128]{2,1,3,0:T(8,128)(2,1)} %copy.81, bf16[5,18,8,128]{2,1,3,0:T(8,128)(2,1)} %copy.80, bf16[5,18,5,128]{2,1,3,0:T(8,128)(2,1)} %copy.79), kind=kLoop, calls=%fused_computation.1 | loop fusion | flops 1244160 | bytes 829440 | tf_op jit(solution)/shard_map/concatenate | solution.py:19
  88.1 1.9 %copy-done = bf16[5,18,18,128]{2,1,3,0:T(8,128)(2,1)} copy-done((bf16[5,18,18,128]{2,1,3,0:T(8,128)(2,1)}, bf16[5,18,18,128]{2,1,3,0:T(8,128)(2,1)S(1)}, u32[]{:S(2)}) %copy-start) | copy-done | bytes 414744
  90.0 1.6 %collective-permute-start.16 = (bf16[5,18,18,5]{2,1,3,0:T(8,128)(2,1)S(1)}, bf16[5,18,18,5]{2,1,3,0:T(8,128)(2,1)S(1)}, u32[]{:S(2)}, u32[]{:S(2)}) collective-permute-start(bf16[5,18,18,5]{2,1,3,0:T(8,128)(2,1)S(1)} %get-tuple-element.26), channel_id=1, source_target_pairs={{0,1},{1,0},{2,3},{3,2},{4,5},{5,4},{6,7},{7,6},{8,9},{9,8},{10,11... | collective-permute-start | bytes 48608 | tf_op jit(solution)/shard_map/ppermute | solution.py:21
  92.5 4.7 %copy.83 = bf16[5,18,18,128]{3,2,1,0:T(8,128)(2,1)S(1)} copy(bf16[5,18,18,128]{2,1,3,0:T(8,128)(2,1)} %copy-done) | data formatting | bytes 829440 | tf_op jit(solution)/shard_map/concatenate | solution.py:19
  (211 shorter events, 31.3 us)
Async XLA Ops:
  1.4 9.1 %collective-permute-start.6 = (f32[5,8,128]{2,1,0:T(8,128)S(1)}, f32[5,8,128]{2,1,0:T(8,128)S(1)}, u32[]{:S(2)}, u32[]{:S(2)}) collective-permute-start(f32[5,8,128]{2,1,0:T(8,128)S(1)} %get-tuple-element.99), channel_id=1, source_target_pairs={{0,4},{4,8},{8,12},{12,16},{16,20},{20,24},{24,28},{28,0},{1,5},{5... | collective-permute-start | bytes 61448 | tf_op jit(solution)/shard_map/ppermute | solution.py:21
  5.3 9.3 %collective-permute-start = (bf16[5,5,8,128]{3,2,1,0:T(8,128)(2,1)S(1)}, bf16[5,5,8,128]{3,2,1,0:T(8,128)(2,1)S(1)}, u32[]{:S(2)}, u32[]{:S(2)}) collective-permute-start(bf16[5,5,8,128]{3,2,1,0:T(8,128)(2,1)S(1)} %get-tuple-element.93), channel_id=1, source_target_pairs={{0,4},{4,8},{8,12},{12,16},{16,20},{20,24},{24,28},{28,0},{1,5},{5... | collective-permute-start | bytes 153608 | tf_op jit(solution)/shard_map/ppermute | solution.py:21
  6.9 8.6 %collective-permute-start.1 = (bf16[5,5,8,128]{3,2,1,0:T(8,128)(2,1)S(1)}, bf16[5,5,8,128]{3,2,1,0:T(8,128)(2,1)S(1)}, u32[]{:S(2)}, u32[]{:S(2)}) collective-permute-start(bf16[5,5,8,128]{3,2,1,0:T(8,128)(2,1)S(1)} %get-tuple-element.92), channel_id=1, source_target_pairs={{4,0},{8,4},{12,8},{16,12},{20,16},{24,20},{28,24},{0,28},{5,1},{9... | collective-permute-start | bytes 153608 | tf_op jit(solution)/shard_map/ppermute | solution.py:23
  10.1 3.8 %collective-permute-start.7 = (f32[5,8,128]{2,1,0:T(8,128)S(1)}, f32[5,8,128]{2,1,0:T(8,128)S(1)}, u32[]{:S(2)}, u32[]{:S(2)}) collective-permute-start(f32[5,8,128]{2,1,0:T(8,128)S(1)} %get-tuple-element.98), channel_id=1, source_target_pairs={{4,0},{8,4},{12,8},{16,12},{20,16},{24,20},{28,24},{0,28},{5,1},{9... | collective-permute-start | bytes 61448 | tf_op jit(solution)/shard_map/ppermute | solution.py:23
  13.9 5.8 %collective-permute-start.8 = (f32[18,5,128]{2,0,1:T(8,128)S(1)}, f32[18,5,128]{2,0,1:T(8,128)S(1)}, u32[]{:S(2)}, u32[]{:S(2)}) collective-permute-start(f32[18,5,128]{2,0,1:T(8,128)S(1)} %copy.91), channel_id=1, source_target_pairs={{0,2},{2,0},{1,3},{3,1},{4,6},{6,4},{5,7},{7,5},{8,10},{10,8},{9,1... | collective-permute-start | bytes 138248 | tf_op jit(solution)/shard_map/ppermute | solution.py:21
  14.0 5.8 %collective-permute-start.9 = (f32[18,5,128]{2,0,1:T(8,128)S(1)}, f32[18,5,128]{2,0,1:T(8,128)S(1)}, u32[]{:S(2)}, u32[]{:S(2)}) collective-permute-start(f32[18,5,128]{2,0,1:T(8,128)S(1)} %copy.92), channel_id=1, source_target_pairs={{2,0},{0,2},{3,1},{1,3},{6,4},{4,6},{7,5},{5,7},{10,8},{8,10},{11,... | collective-permute-start | bytes 138248 | tf_op jit(solution)/shard_map/ppermute | solution.py:23
  19.1 3.0 %collective-permute-start.2 = (bf16[5,18,5,128]{3,1,2,0:T(8,128)(2,1)S(1)}, bf16[5,18,5,128]{3,1,2,0:T(8,128)(2,1)S(1)}, u32[]{:S(2)}, u32[]{:S(2)}) collective-permute-start(bf16[5,18,5,128]{3,1,2,0:T(8,128)(2,1)S(1)} %copy.89), channel_id=1, source_target_pairs={{0,2},{2,0},{1,3},{3,1},{4,6},{6,4},{5,7},{7,5},{8,10},{10,8},{9,1... | collective-permute-start | bytes 345608 | tf_op jit(solution)/shard_map/ppermute | solution.py:21
  19.2 6.4 %collective-permute-start.3 = (bf16[5,18,5,128]{3,1,2,0:T(8,128)(2,1)S(1)}, bf16[5,18,5,128]{3,1,2,0:T(8,128)(2,1)S(1)}, u32[]{:S(2)}, u32[]{:S(2)}) collective-permute-start(bf16[5,18,5,128]{3,1,2,0:T(8,128)(2,1)S(1)} %copy.90), channel_id=1, source_target_pairs={{2,0},{0,2},{3,1},{1,3},{6,4},{4,6},{7,5},{5,7},{10,8},{8,10},{11,... | collective-permute-start | bytes 345608 | tf_op jit(solution)/shard_map/ppermute | solution.py:23
  20.0 19.8 %collective-permute-start.10 = (f32[18,18,5]{2,1,0:T(8,128)S(1)}, f32[18,18,5]{2,1,0:T(8,128)S(1)}, u32[]{:S(2)}, u32[]{:S(2)}) collective-permute-start(f32[18,18,5]{2,1,0:T(8,128)S(1)} %get-tuple-element.64), channel_id=1, source_target_pairs={{0,1},{1,0},{2,3},{3,2},{4,5},{5,4},{6,7},{7,6},{8,9},{9,8},{10,11... | collective-permute-start | bytes 19448 | tf_op jit(solution)/shard_map/ppermute | solution.py:21
  21.5 18.3 %collective-permute-start.11 = (f32[18,18,5]{2,1,0:T(8,128)S(1)}, f32[18,18,5]{2,1,0:T(8,128)S(1)}, u32[]{:S(2)}, u32[]{:S(2)}) collective-permute-start(f32[18,18,5]{2,1,0:T(8,128)S(1)} %get-tuple-element.65), channel_id=1, source_target_pairs={{1,0},{0,1},{3,2},{2,3},{5,4},{4,5},{7,6},{6,7},{9,8},{8,9},{11,10... | collective-permute-start | bytes 19448 | tf_op jit(solution)/shard_map/ppermute | solution.py:23
  37.7 7.0 %collective-permute-start.4 = (bf16[5,18,18,5]{2,1,3,0:T(8,128)(2,1)S(1)}, bf16[5,18,18,5]{2,1,3,0:T(8,128)(2,1)S(1)}, u32[]{:S(2)}, u32[]{:S(2)}) collective-permute-start(bf16[5,18,18,5]{2,1,3,0:T(8,128)(2,1)S(1)} %get-tuple-element.28), channel_id=1, source_target_pairs={{0,1},{1,0},{2,3},{3,2},{4,5},{5,4},{6,7},{7,6},{8,9},{9,8},{10,11... | collective-permute-start | bytes 48608 | tf_op jit(solution)/shard_map/ppermute | solution.py:21
  39.3 7.2 %collective-permute-start.5 = (bf16[5,18,18,5]{2,1,3,0:T(8,128)(2,1)S(1)}, bf16[5,18,18,5]{2,1,3,0:T(8,128)(2,1)S(1)}, u32[]{:S(2)}, u32[]{:S(2)}) collective-permute-start(bf16[5,18,18,5]{2,1,3,0:T(8,128)(2,1)S(1)} %get-tuple-element.29), channel_id=1, source_target_pairs={{1,0},{0,1},{3,2},{2,3},{5,4},{4,5},{7,6},{6,7},{9,8},{8,9},{11,10... | collective-permute-start | bytes 48608 | tf_op jit(solution)/shard_map/ppermute | solution.py:23
  55.7 9.8 %collective-permute-start.18 = (f32[5,8,128]{2,1,0:T(8,128)S(1)}, f32[5,8,128]{2,1,0:T(8,128)S(1)}, u32[]{:S(2)}, u32[]{:S(2)}) collective-permute-start(f32[5,8,128]{2,1,0:T(8,128)S(1)} %get-tuple-element.88), channel_id=1, source_target_pairs={{0,4},{4,8},{8,12},{12,16},{16,20},{20,24},{24,28},{28,0},{1,5},{5... | collective-permute-start | bytes 61448 | tf_op jit(solution)/shard_map/ppermute | solution.py:21
  55.8 9.7 %collective-permute-start.19 = (f32[5,8,128]{2,1,0:T(8,128)S(1)}, f32[5,8,128]{2,1,0:T(8,128)S(1)}, u32[]{:S(2)}, u32[]{:S(2)}) collective-permute-start(f32[5,8,128]{2,1,0:T(8,128)S(1)} %get-tuple-element.89), channel_id=1, source_target_pairs={{4,0},{8,4},{12,8},{16,12},{20,16},{24,20},{28,24},{0,28},{5,1},{9... | collective-permute-start | bytes 61448 | tf_op jit(solution)/shard_map/ppermute | solution.py:23
  60.7 6.9 %collective-permute-start.12 = (bf16[5,5,8,128]{3,2,1,0:T(8,128)(2,1)S(1)}, bf16[5,5,8,128]{3,2,1,0:T(8,128)(2,1)S(1)}, u32[]{:S(2)}, u32[]{:S(2)}) collective-permute-start(bf16[5,5,8,128]{3,2,1,0:T(8,128)(2,1)S(1)} %get-tuple-element.90), channel_id=1, source_target_pairs={{0,4},{4,8},{8,12},{12,16},{16,20},{20,24},{24,28},{28,0},{1,5},{5... | collective-permute-start | bytes 153608 | tf_op jit(solution)/shard_map/ppermute | solution.py:21
  60.8 6.8 %collective-permute-start.13 = (bf16[5,5,8,128]{3,2,1,0:T(8,128)(2,1)S(1)}, bf16[5,5,8,128]{3,2,1,0:T(8,128)(2,1)S(1)}, u32[]{:S(2)}, u32[]{:S(2)}) collective-permute-start(bf16[5,5,8,128]{3,2,1,0:T(8,128)(2,1)S(1)} %get-tuple-element.91), channel_id=1, source_target_pairs={{4,0},{8,4},{12,8},{16,12},{20,16},{24,20},{28,24},{0,28},{5,1},{9... | collective-permute-start | bytes 153608 | tf_op jit(solution)/shard_map/ppermute | solution.py:23
  65.6 6.5 %collective-permute-start.20 = (f32[18,5,128]{2,0,1:T(8,128)S(1)}, f32[18,5,128]{2,0,1:T(8,128)S(1)}, u32[]{:S(2)}, u32[]{:S(2)}) collective-permute-start(f32[18,5,128]{2,0,1:T(8,128)S(1)} %copy.95), channel_id=1, source_target_pairs={{0,2},{2,0},{1,3},{3,1},{4,6},{6,4},{5,7},{7,5},{8,10},{10,8},{9,1... | collective-permute-start | bytes 138248 | tf_op jit(solution)/shard_map/ppermute | solution.py:21
  65.7 6.4 %collective-permute-start.21 = (f32[18,5,128]{2,0,1:T(8,128)S(1)}, f32[18,5,128]{2,0,1:T(8,128)S(1)}, u32[]{:S(2)}, u32[]{:S(2)}) collective-permute-start(f32[18,5,128]{2,0,1:T(8,128)S(1)} %copy.96), channel_id=1, source_target_pairs={{2,0},{0,2},{3,1},{1,3},{6,4},{4,6},{7,5},{5,7},{10,8},{8,10},{11,... | collective-permute-start | bytes 138248 | tf_op jit(solution)/shard_map/ppermute | solution.py:23
  71.4 3.0 %collective-permute-start.14 = (bf16[5,18,5,128]{3,1,2,0:T(8,128)(2,1)S(1)}, bf16[5,18,5,128]{3,1,2,0:T(8,128)(2,1)S(1)}, u32[]{:S(2)}, u32[]{:S(2)}) collective-permute-start(bf16[5,18,5,128]{3,1,2,0:T(8,128)(2,1)S(1)} %copy.93), channel_id=1, source_target_pairs={{0,2},{2,0},{1,3},{3,1},{4,6},{6,4},{5,7},{7,5},{8,10},{10,8},{9,1... | collective-permute-start | bytes 345608 | tf_op jit(solution)/shard_map/ppermute | solution.py:21
  71.5 6.5 %collective-permute-start.15 = (bf16[5,18,5,128]{3,1,2,0:T(8,128)(2,1)S(1)}, bf16[5,18,5,128]{3,1,2,0:T(8,128)(2,1)S(1)}, u32[]{:S(2)}, u32[]{:S(2)}) collective-permute-start(bf16[5,18,5,128]{3,1,2,0:T(8,128)(2,1)S(1)} %copy.94), channel_id=1, source_target_pairs={{2,0},{0,2},{3,1},{1,3},{6,4},{4,6},{7,5},{5,7},{10,8},{8,10},{11,... | collective-permute-start | bytes 345608 | tf_op jit(solution)/shard_map/ppermute | solution.py:23
  72.3 19.8 %collective-permute-start.22 = (f32[18,18,5]{2,1,0:T(8,128)S(1)}, f32[18,18,5]{2,1,0:T(8,128)S(1)}, u32[]{:S(2)}, u32[]{:S(2)}) collective-permute-start(f32[18,18,5]{2,1,0:T(8,128)S(1)} %get-tuple-element.62), channel_id=1, source_target_pairs={{0,1},{1,0},{2,3},{3,2},{4,5},{5,4},{6,7},{7,6},{8,9},{9,8},{10,11... | collective-permute-start | bytes 19448 | tf_op jit(solution)/shard_map/ppermute | solution.py:21
  73.8 18.3 %collective-permute-start.23 = (f32[18,18,5]{2,1,0:T(8,128)S(1)}, f32[18,18,5]{2,1,0:T(8,128)S(1)}, u32[]{:S(2)}, u32[]{:S(2)}) collective-permute-start(f32[18,18,5]{2,1,0:T(8,128)S(1)} %get-tuple-element.63), channel_id=1, source_target_pairs={{1,0},{0,1},{3,2},{2,3},{5,4},{4,5},{7,6},{6,7},{9,8},{8,9},{11,10... | collective-permute-start | bytes 19448 | tf_op jit(solution)/shard_map/ppermute | solution.py:23
  90.0 7.1 %collective-permute-start.16 = (bf16[5,18,18,5]{2,1,3,0:T(8,128)(2,1)S(1)}, bf16[5,18,18,5]{2,1,3,0:T(8,128)(2,1)S(1)}, u32[]{:S(2)}, u32[]{:S(2)}) collective-permute-start(bf16[5,18,18,5]{2,1,3,0:T(8,128)(2,1)S(1)} %get-tuple-element.26), channel_id=1, source_target_pairs={{0,1},{1,0},{2,3},{3,2},{4,5},{5,4},{6,7},{7,6},{8,9},{9,8},{10,11... | collective-permute-start | bytes 48608 | tf_op jit(solution)/shard_map/ppermute | solution.py:21
  91.6 7.2 %collective-permute-start.17 = (bf16[5,18,18,5]{2,1,3,0:T(8,128)(2,1)S(1)}, bf16[5,18,18,5]{2,1,3,0:T(8,128)(2,1)S(1)}, u32[]{:S(2)}, u32[]{:S(2)}) collective-permute-start(bf16[5,18,18,5]{2,1,3,0:T(8,128)(2,1)S(1)} %get-tuple-element.27), channel_id=1, source_target_pairs={{1,0},{0,1},{3,2},{2,3},{5,4},{4,5},{7,6},{6,7},{9,8},{8,9},{11,10... | collective-permute-start | bytes 48608 | tf_op jit(solution)/shard_map/ppermute | solution.py:23
  (3 other events, 9.1 us)
where the time goes:
time: 110 us; the launch traced here: 109 us
  local copies, waits for them, and re-layouts  41.5 us (38%)
  other arithmetic  31.5 us (29%)
  starting transfers between devices  28.6 us (26%)
  waiting for transfers between devices  5.92 us (5%)
  between operations  1.77 us (2%)
    ppermute x12, starting transfers between devices, extended(): lax.ppermute(head, axis, [((i + 1) % count, i) for i in range(count)])  17.4 us
    concatenate x6, local copies, waits for them, and re-layouts, extended(): jnp.concatenate([lax.ppermute(tail, axis, [(i, (i + 1) % count) for i in...  16.4 us
    concatenate x8, other arithmetic, extended(): jnp.concatenate([lax.ppermute(tail, axis, [(i, (i + 1) % count) for i in...  13.9 us
    ppermute x12, starting transfers between devices, extended(): lax.ppermute(tail, axis, [(i, (i + 1) % count) for i in range(count)])  11.2 us
    ppermute x6, local copies, waits for them, and re-layouts, extended(): lax.ppermute(tail, axis, [(i, (i + 1) % count) for i in range(count)])  8.58 us
    ppermute x6, local copies, waits for them, and re-layouts, extended(): lax.ppermute(head, axis, [((i + 1) % count, i) for i in range(count)])  8.53 us
    div x8, other arithmetic, sweep(): return numerator / denominator  6.94 us
    unnamed x22, local copies, waits for them, and re-layouts  5.62 us
  transfers between devices with their start and end apart: 24, of which 4 were waited for; matrix products, arithmetic and copies ran while one was open for 45% of the time, Pallas kernels for 0%

commit v1 on v0

v1 whole, which is shorter than its diff:
```python
import functools

import jax
import jax.numpy as jnp
from jax import lax
from jax.experimental import pallas as pl
from jax.experimental.pallas import tpu as pltpu
from jax.sharding import PartitionSpec as P

SWEEPS = 4
HALO = SWEEPS + 1
REACH = 3
gamma_gas = 1.4
alpha_reg = 4.0
time_step = 0.08
MESH = pl.DeviceIdType.MESH
F32 = jnp.float32
BF16 = jnp.bfloat16


def edges(c, p1, m1, p2, m2):
    even = (47.0 / 60.0) * c + (7.0 / 60.0) * (p1 + m1) - (0.5 / 60.0) * (p2 + m2)
    odd = (20.0 / 60.0) * (p1 - m1) - (2.5 / 60.0) * (p2 - m2)
    return even + odd, even - odd


def physical_flux(v, d):
    inv = 1.0 / v[0]
    u = [v[1] * inv, v[2] * inv, v[3] * inv]
    kinetic = 0.5 * (v[1] * u[0] + v[2] * u[1] + v[3] * u[2])
    p = (gamma_gas - 1.0) * (v[4] - kinetic)
    n = u[d]
    flux = [v[1 + d], v[1] * n, v[2] * n, v[3] * n, (v[4] + p) * n]
    flux[1 + d] = flux[1 + d] + p
    return flux, jnp.abs(n) + jnp.sqrt(gamma_gas * jnp.abs(p) * inv)


def face_flux(left, right, d):
    fl, sl = physical_flux(left, d)
    fr, sr = physical_flux(right, d)
    speed = jnp.maximum(sl, sr)
    return [0.5 * ((a + b) - speed * (r - l)) for a, b, l, r in zip(fl, fr, left, right)]


def up(v, axis, by=1):
    return pltpu.roll(v, (v.shape[axis] - by) % v.shape[axis], axis)


def down(v, axis, by=1):
    return pltpu.roll(v, by, axis)


def kernel(counts, cons, sigma, new_out, ent_out, xq, xe, xs, yq, ys, yxq, yxs, pq, ps, rq, rs,
           st1, sg1, QF, U, INV, CO, SA, SB, T, send_sem, recv_sem):
    gx, gy, gz = lax.axis_index("gx"), lax.axis_index("gy"), lax.axis_index("gz")
    nx, ny, nz = sigma.shape
    px = nx + 2 * HALO
    slot = nz // nx
    own_y, own_z = slice(0, ny), slice(0, nz)
    far_y, far_z = slice(ny, 2 * ny), slice(nz, 2 * nz)

    def dev(dx, dy, dz):
        return (
            lax.rem(gx + dx + counts[0], counts[0]),
            lax.rem(gy + dy, counts[1]),
            lax.rem(gz + dz, counts[2]),
        )

    lane = lax.broadcasted_iota(jnp.int32, (ny, nz), 1)

    def pack(sec, q, s):
        for f in range(6):
            acc = None
            for k in range(nx):
                v = q[f, k].astype(F32) if f < 5 else s[k]
                r = pltpu.roll(v, (HALO + slot * k) % nz, 1)
                acc = r if acc is None else jnp.where(lane >= slot * k, r, acc)
            if f < 5:
                pq[sec, f] = acc.astype(BF16)
            else:
                ps[sec] = acc

    peers = [(-1, 0, 0), (1, 0, 0), (0, 1, 0)] + [
        (dx, dy, 1) for dx in (0, -1, 1) for dy in (0, 1)
    ]

    def section(sec, q, s):
        number = [0]

        def copy(src, dst, where):
            k = number[0]
            number[0] += 1
            return pltpu.make_async_remote_copy(
                src_ref=src, dst_ref=dst, send_sem=send_sem.at[sec, k],
                recv_sem=recv_sem.at[sec, k], device_id=dev(*where), device_id_type=MESH,
            )

        x_copies = []
        for side in (0, 1):
            to = (1, 0, 0) if side == 0 else (-1, 0, 0)
            a = nx - HALO if side == 0 else 0
            b = nx - REACH if side == 0 else 0
            x_copies.append([
                copy(q.at[0:4, a:a + HALO], xq.at[sec, side], to),
                copy(s.at[a:a + HALO], xs.at[sec, side], to),
                copy(q.at[4, b:b + REACH], xe.at[sec, side], to),
            ])
        y_copies = [copy(q, yq.at[sec], (0, 1, 0)), copy(s, ys.at[sec], (0, 1, 0))]
        relays = [
            [copy(xq.at[sec, side], yxq.at[sec, side], (0, 1, 0)),
             copy(xs.at[sec, side], yxs.at[sec, side], (0, 1, 0))]
            for side in (0, 1)
        ]
        z_copies = {}
        for dx, dy, dz in peers[3:]:
            z_copies[(1 - dx, dy)] = [
                copy(pq.at[sec], rq.at[sec, 1 - dx, dy], (dx, dy, dz)),
                copy(ps.at[sec], rs.at[sec, 1 - dx, dy], (dx, dy, dz)),
            ]
        everything = x_copies[0] + x_copies[1] + y_copies + relays[0] + relays[1]
        for both in z_copies.values():
            everything = everything + both

        for pair in x_copies:
            for c in pair:
                c.start()
        for c in y_copies:
            c.start()
        if sec == 1:
            pack(sec, q, s)
        for both in z_copies.values():
            for c in both:
                c.start()

        for k in range(nx):
            for f in range(5):
                QF[f, HALO + k, own_y, own_z] = q[f, k].astype(F32)
            SA[HALO + k, own_y, own_z] = s[k]

        def unpack(j, dy, k, plane, fields):
            rows = far_y if dy else own_y
            back = (nz - (HALO + slot * k) % nz) % nz
            for f in range(fields):
                QF[f, plane, rows, far_z] = pltpu.roll(rq[sec, j, dy, f].astype(F32), back, 1)
            SA[plane, rows, far_z] = pltpu.roll(rs[sec, j, dy], back, 1)

        for c in y_copies:
            c.wait_recv()
        for k in range(nx):
            for f in range(5):
                QF[f, HALO + k, far_y, own_z] = yq[sec, f, k].astype(F32)
            SA[HALO + k, far_y, own_z] = ys[sec, k]
        for dy in (0, 1):
            for c in z_copies[(1, dy)]:
                c.wait_recv()
            for k in range(nx):
                unpack(1, dy, k, HALO + k, 5)

        def side_flux(k, carry):
            p = HALO + k
            total = None
            for d, axis, rows, cols in ((1, 0, slice(0, 2 * ny), own_z), (2, 1, own_y, slice(0, 2 * nz))):
                left, right = [], []
                for f in range(5):
                    c = QF[f, p, rows, cols]
                    l, r = edges(c, up(c, axis), down(c, axis), up(c, axis, 2), down(c, axis, 2))
                    left.append(l)
                    right.append(up(r, axis))
                h = face_flux(left, right, d)
                change = [(v - down(v, axis))[own_y, own_z] for v in h]
                total = change if total is None else [a + b for a, b in zip(total, change)]
            for f in range(5):
                T[f, k] = total[f]
            return carry

        lax.fori_loop(0, nx, side_flux, 0)

        for side in (0, 1):
            for c in x_copies[side]:
                c.wait_recv()
            for c in relays[side]:
                c.start()
        for side in (0, 1):
            base = 0 if side == 0 else HALO + nx
            ebase = HALO - REACH if side == 0 else HALO + nx
            for k in range(HALO):
                for f in range(4):
                    QF[f, base + k, own_y, own_z] = xq[sec, side, f, k].astype(F32)
                SA[base + k, own_y, own_z] = xs[sec, side, k]
            for k in range(REACH):
                QF[4, ebase + k, own_y, own_z] = xe[sec, side, k].astype(F32)

        def x_face(p):
            left, right = [], []
            for f in range(5):
                v = [QF[f, p + o, own_y, own_z] for o in range(-2, 4)]
                left.append(edges(v[2], v[3], v[1], v[4], v[0])[0])
                right.append(edges(v[3], v[4], v[2], v[5], v[1])[1])
            return face_flux(left, right, 0)

        def x_flux(k, before):
            h = x_face(HALO + k)
            for f in range(5):
                T[f, k] = T[f, k] + (h[f] - before[f])
            return tuple(h)

        lax.fori_loop(0, nx, x_flux, tuple(x_face(HALO - 1)), unroll=2)

        for side in (0, 1):
            j = 0 if side == 0 else 2
            base = 0 if side == 0 else HALO + nx
            first = nx - HALO if side == 0 else 0
            for dy in (0, 1):
                for c in z_copies[(j, dy)]:
                    c.wait_recv()
                for k in range(HALO):
                    unpack(j, dy, first + k, base + k, 4)
        for side in (0, 1):
            base = 0 if side == 0 else HALO + nx
            for c in relays[side]:
                c.wait_recv()
            for k in range(HALO):
                for f in range(4):
                    QF[f, base + k, far_y, own_z] = yxq[sec, side, f, k].astype(F32)
                SA[base + k, far_y, own_z] = yxs[sec, side, k]

        def velocities(p, carry):
            inv = 1.0 / QF[0, p]
            INV[p] = inv
            for a in range(3):
                U[a, p] = QF[1 + a, p] * inv
            return carry

        lax.fori_loop(0, px, velocities, 0, unroll=2)

        def coefficients(p, carry):
            g = []
            for a in range(3):
                u = U[a, p]
                g.append([
                    U[a, p + 1] - U[a, p - 1], up(u, 0) - down(u, 0), up(u, 1) - down(u, 1),
                ])
            div = g[0][0] + g[1][1] + g[2][2]
            total = div * div + g[0][0] * g[0][0] + g[1][1] * g[1][1] + g[2][2] * g[2][2]
            total = total + 2.0 * (g[0][1] * g[1][0] + g[0][2] * g[2][0] + g[1][2] * g[2][1])
            source = (alpha_reg * 0.25) * total
            c = INV[p]
            around = [INV[p + 1], INV[p - 1], up(c, 0), down(c, 0), up(c, 1), down(c, 1)]
            w = [(alpha_reg * 0.5) * (c + n) for n in around]
            scale = 1.0 / (c + ((w[0] + w[1]) + (w[2] + w[3]) + (w[4] + w[5])))
            for n in range(6):
                CO[n, p] = w[n] * scale
            CO[6, p] = source * scale
            return carry

        lax.fori_loop(1, px - 1, coefficients, 0)

        read, write = SA, SB
        for step in range(SWEEPS):
            def one(p, carry, read=read, write=write):
                c = read[p]
                out = CO[6, p] + CO[0, p] * read[p + 1] + CO[1, p] * read[p - 1]
                out = out + (CO[2, p] * up(c, 0) + CO[3, p] * down(c, 0))
                out = out + (CO[4, p] * up(c, 1) + CO[5, p] * down(c, 1))
                write[p] = out
                return carry

            lax.fori_loop(step + 1, px - 1 - step, one, 0, unroll=2)
            read, write = write, read
        S = read

        def finish(k, carry):
            p = HALO + k
            tile = (own_y, own_z)
            push = [T[f, k] for f in range(5)]
            xp, xm = S[(p + 1,) + tile], S[(p - 1,) + tile]
            push[1] = push[1] + 0.5 * (xp - xm)
            power = xp * U[(0, p + 1) + tile] - xm * U[(0, p - 1) + tile]
            sy = S[p, :, own_z]
            push[2] = push[2] + 0.5 * (up(sy, 0) - down(sy, 0))[own_y, own_z]
            e = sy * U[1, p, :, own_z]
            power = power + (up(e, 0) - down(e, 0))[own_y, own_z]
            sz = S[p, own_y, :]
            push[3] = push[3] + 0.5 * (up(sz, 1) - down(sz, 1))[own_y, own_z]
            e = sz * U[2, p, own_y, :]
            power = power + (up(e, 1) - down(e, 1))[own_y, own_z]
            push[4] = push[4] + 0.5 * power
            for f in range(5):
                initial = cons[f, k].astype(F32)
                moved = initial - time_step * push[f]
                if sec == 0:
                    st1[f, k] = moved.astype(BF16)
                else:
                    new_out[f, k] = 0.5 * (moved + st1[f, k].astype(F32))
            mid = S[(p,) + tile]
            if sec == 0:
                sg1[k] = mid
            else:
                ent_out[k] = mid
            return carry

        lax.fori_loop(0, nx, finish, 0, unroll=2)
        return everything

    pack(0, cons, sigma)
    barrier = pltpu.get_barrier_semaphore()
    for peer in peers:
        pl.semaphore_signal(barrier, inc=1, device_id=dev(*peer), device_id_type=MESH)
    pl.semaphore_wait(barrier, len(peers))
    first = section(0, cons, sigma)
    second = section(1, st1, sg1)
    for c in first + second:
        c.wait_send()


def solution(mesh):
    counts = (mesh.shape["gx"], mesh.shape["gy"], mesh.shape["gz"])
    assert counts[1] == 2 and counts[2] == 2

    def step(conserved, sigma_prev):
        _, nx, ny, nz = conserved.shape
        px = nx + 2 * HALO
        wide = (2 * ny, 2 * nz)
        vmem = pl.BlockSpec(memory_space=pltpu.VMEM)
        return pl.pallas_call(
            functools.partial(kernel, counts),
            out_shape=(
                jax.ShapeDtypeStruct((5, nx, ny, nz), F32),
                jax.ShapeDtypeStruct((nx, ny, nz), F32),
            ),
            in_specs=[vmem, vmem],
            out_specs=(vmem, vmem),
            scratch_shapes=[
                pltpu.VMEM((2, 2, 4, HALO, ny, nz), BF16),
                pltpu.VMEM((2, 2, REACH, ny, nz), BF16),
                pltpu.VMEM((2, 2, HALO, ny, nz), F32),
                pltpu.VMEM((2, 5, nx, ny, nz), BF16),
                pltpu.VMEM((2, nx, ny, nz), F32),
                pltpu.VMEM((2, 2, 4, HALO, ny, nz), BF16),
                pltpu.VMEM((2, 2, HALO, ny, nz), F32),
                pltpu.VMEM((2, 5, ny, nz), BF16),
                pltpu.VMEM((2, ny, nz), F32),
                pltpu.VMEM((2, 3, 2, 5, ny, nz), BF16),
                pltpu.VMEM((2, 3, 2, ny, nz), F32),
                pltpu.VMEM((5, nx, ny, nz), BF16),
                pltpu.VMEM((nx, ny, nz), F32),
                pltpu.VMEM((5, px) + wide, F32),
                pltpu.VMEM((3, px) + wide, F32),
                pltpu.VMEM((px,) + wide, F32),
                pltpu.VMEM((7, px) + wide, F32),
                pltpu.VMEM((px,) + wide, F32),
                pltpu.VMEM((px,) + wide, F32),
                pltpu.VMEM((5, nx, ny, nz), F32),
                pltpu.SemaphoreType.DMA((2, 24)),
                pltpu.SemaphoreType.DMA((2, 24)),
            ],
            compiler_params=pltpu.CompilerParams(collective_id=0, has_side_effects=True),
        )(conserved, sigma_prev)

    return jax.shard_map(
        step,
        mesh=mesh,
        in_specs=(P(None, "gx", "gy", "gz"), P("gx", "gy", "gz")),
        out_specs=(P(None, "gx", "gy", "gz"), P("gx", "gy", "gz")),
        check_vma=False,
    )
```

time: 110 us -> 35 us (0.32)
  local copies, waits for them, and re-layouts: 41.5 us -> 2.22 us
  Pallas kernels: 0 us -> 31.9 us
  other arithmetic: 31.5 us -> 0 us
  starting transfers between devices: 28.6 us -> 0 us
  waiting for transfers between devices: 5.92 us -> 0 us
  between operations: 1.77 us -> 0.65 us
    pallas_call x0 -> x1, Pallas kernels: none -> 31.9 us  [step(): pl.pallas_call(functools.partial(kernel, counts), out_shape=(jax.ShapeDty...]
    ppermute x24 -> x0, starting transfers between devices: 28.6 us -> none  [the longest x12 17.4 us: extended(): lax.ppermute(head, axis, [((i + 1) % count, i) for i in range(count)])]
    ppermute x12 -> x0, local copies, waits for them, and re-layouts: 17.1 us -> none  [the longest x6 8.58 us: extended(): lax.ppermute(tail, axis, [(i, (i + 1) % count) for i in range(count)])]
    concatenate x6 -> x0, local copies, waits for them, and re-layouts: 16.4 us -> none  [extended(): jnp.concatenate([lax.ppermute(tail, axis, [(i, (i + 1) % count) for i in...]
    concatenate x8 -> x0, other arithmetic: 13.9 us -> none  [extended(): jnp.concatenate([lax.ppermute(tail, axis, [(i, (i + 1) % count) for i in...]
    div x28 -> x0, other arithmetic: 10.6 us -> none  [the longest x8 6.94 us: sweep(): return numerator / denominator]
    ppermute x24 -> x0, waiting for transfers between devices: 5.92 us -> none  [the longest x12 4.52 us: extended(): lax.ppermute(head, axis, [((i + 1) % count, i) for i in range(count)])]
    unnamed x22 -> x4, local copies, waits for them, and re-layouts: 5.62 us -> 2.22 us
  transfers between devices with their start and end apart: 24 -> 0, of which waited for: 4 -> 0; matrix products, arithmetic and copies ran while one was open for 45% -> 0% of each run, Pallas kernels for 0% -> 0%
where the time goes in v1:
time: 35 us; the launch traced here: 34.8 us
  Pallas kernels  31.9 us (91%)
  local copies, waits for them, and re-layouts  2.22 us (6%)
  between operations  0.65 us (2%)
    pallas_call x1, Pallas kernels, step(): pl.pallas_call(functools.partial(kernel, counts), out_shape=(jax.ShapeDty...  31.9 us
    unnamed x4, local copies, waits for them, and re-layouts  2.22 us

profile of v1, /device:TPU:0, one launch (start us, length us, event | category | flops | bytes accessed | tf_op | source)
XLA Modules:
  0.0 34.8 jit_solution(14353689439944484855)
XLA Ops:
  0.6 31.9 %shard_map.41 = (f32[5,8,8,128]{3,2,1,0:T(8,128)}, f32[8,8,128]{2,1,0:T(8,128)}) custom-call(bf16[5,8,8,128]{3,2,1,0:T(8,128)(2,1)} %cons.1, f32[8,8,128]{2,1,0:T(8,128)} %sigma.1), custom_call_target="tpu_custom_call" | custom-call | tf_op jit(solution)/shard_map/pallas_call | solution.py:325
  32.6 0.0 copy-start
  32.6 1.6 %copy.6 = f32[5,8,8,128]{3,2,1,0:T(8,128)} copy(f32[5,8,8,128]{3,2,1,0:T(8,128)} %get-tuple-element.4) | data formatting | bytes 327680
  34.2 0.0 copy-done
  34.2 0.6 %copy.7 = f32[8,8,128]{2,1,0:T(8,128)} copy(f32[8,8,128]{2,1,0:T(8,128)S(1)} %copy-done) | data formatting | bytes 65536
Async XLA Ops:
  32.6 1.6 %copy-start = (f32[8,8,128]{2,1,0:T(8,128)S(1)}, f32[8,8,128]{2,1,0:T(8,128)}, u32[]{:S(2)}) copy-start(f32[8,8,128]{2,1,0:T(8,128)} %get-tuple-element.5) | copy-start | bytes 98308

commit v2 on v1

v2 whole, which is shorter than its diff:
```python
import functools

import jax
import jax.numpy as jnp
from jax import lax
from jax.experimental import pallas as pl
from jax.experimental.pallas import tpu as pltpu
from jax.sharding import PartitionSpec as P

SWEEPS = 4
HALO = SWEEPS + 1
REACH = 3
gamma_gas = 1.4
alpha_reg = 4.0
time_step = 0.08
MESH = pl.DeviceIdType.MESH
F32 = jnp.float32
BF16 = jnp.bfloat16


def edges(c, p1, m1, p2, m2):
    even = (47.0 / 60.0) * c + (7.0 / 60.0) * (p1 + m1) - (0.5 / 60.0) * (p2 + m2)
    odd = (20.0 / 60.0) * (p1 - m1) - (2.5 / 60.0) * (p2 - m2)
    return even + odd, even - odd


def physical_flux(v, d):
    inv = 1.0 / v[0]
    u = [v[1] * inv, v[2] * inv, v[3] * inv]
    kinetic = 0.5 * (v[1] * u[0] + v[2] * u[1] + v[3] * u[2])
    p = (gamma_gas - 1.0) * (v[4] - kinetic)
    n = u[d]
    flux = [v[1 + d], v[1] * n, v[2] * n, v[3] * n, (v[4] + p) * n]
    flux[1 + d] = flux[1 + d] + p
    return flux, jnp.abs(n) + jnp.sqrt(gamma_gas * jnp.abs(p) * inv)


def face_flux(left, right, d):
    fl, sl = physical_flux(left, d)
    fr, sr = physical_flux(right, d)
    speed = jnp.maximum(sl, sr)
    return [0.5 * ((a + b) - speed * (r - l)) for a, b, l, r in zip(fl, fr, left, right)]


def up(v, axis, by=1):
    return pltpu.roll(v, (v.shape[axis] - by) % v.shape[axis], axis)


def down(v, axis, by=1):
    return pltpu.roll(v, by, axis)


def kernel(counts, cons, sigma, new_out, ent_out, xq, xe, xs, yq, ys, yxq, yxs, pq, ps, rq, rs,
           stq, sts, QF, U, INV, CO, SA, SB, WQ, WU, WI, WC, WA, WB, ZB, T, send_sem, recv_sem):
    gx, gy, gz = lax.axis_index("gx"), lax.axis_index("gy"), lax.axis_index("gz")
    nx, ny, nz = sigma.shape
    px = nx + 2 * HALO
    slot = nz // nx
    half = slot // 2
    own_y, far_y = slice(0, ny), slice(ny, 2 * ny)

    def dev(dx, dy, dz):
        return (
            lax.rem(gx + dx + counts[0], counts[0]),
            lax.rem(gy + dy, counts[1]),
            lax.rem(gz + dz, counts[2]),
        )

    lane = lax.broadcasted_iota(jnp.int32, (ny, nz), 1)
    lane2 = lax.broadcasted_iota(jnp.int32, (2 * ny, nz), 1)
    lower = (lane & (slot - 1)) < half
    lower2 = (lane2 & (slot - 1)) < half

    def pack(sec, q, s):
        for f in range(6):
            acc = None
            for k in range(nx):
                v = q[f, k].astype(F32) if f < 5 else s[k]
                r = pltpu.roll(v, (half + slot * k) % nz, 1)
                acc = r if acc is None else jnp.where(lane >= slot * k, r, acc)
            if f < 5:
                pq[sec, f] = acc.astype(BF16)
            else:
                ps[sec] = acc

    peers = [(-1, 0, 0), (1, 0, 0), (0, 1, 0), (0, 0, 1), (0, 1, 1), (-1, 0, 1), (1, 0, 1)]

    def x_next(v, g, after):
        r = up(v, 1, slot)
        return r if after is None else jnp.where(lane2 >= nz - slot, up(after, 1, slot), r)

    def x_prev(v, g, before):
        r = down(v, 1, slot)
        return r if before is None else jnp.where(lane2 < slot, down(before, 1, slot), r)

    def section(sec, carry):
        q, s = stq.at[sec], sts.at[sec]
        number = [0]
        everything = []

        def copy(src, dst, where):
            k = number[0]
            number[0] += 1
            c = pltpu.make_async_remote_copy(
                src_ref=src, dst_ref=dst, send_sem=send_sem.at[sec, k],
                recv_sem=recv_sem.at[sec, k], device_id=dev(*where), device_id_type=MESH,
            )
            everything.append(c)
            return c

        x_copies = []
        for side in (0, 1):
            to = (1, 0, 0) if side == 0 else (-1, 0, 0)
            a = nx - HALO if side == 0 else 0
            b = nx - REACH if side == 0 else 0
            x_copies.append([
                copy(q.at[0:4, a:a + HALO], xq.at[sec, side], to),
                copy(s.at[a:a + HALO], xs.at[sec, side], to),
                copy(q.at[4, b:b + REACH], xe.at[sec, side], to),
            ])
        y_copies = [copy(q, yq.at[sec], (0, 1, 0)), copy(s, ys.at[sec], (0, 1, 0))]
        relays = [
            [copy(xq.at[sec, side], yxq.at[sec, side], (0, 1, 0)),
             copy(xs.at[sec, side], yxs.at[sec, side], (0, 1, 0))]
            for side in (0, 1)
        ]
        packs, pack_relays = {}, {}
        for dx, dy, dz in ((0, 0, 1), (0, 1, 0), (0, 1, 1)):
            packs[(dy, dz, 1)] = [
                copy(pq.at[sec], rq.at[sec, dy, dz, 1], (dx, dy, dz)),
                copy(ps.at[sec], rs.at[sec, dy, dz, 1], (dx, dy, dz)),
            ]
        for dz in (0, 1):
            for dx in (1, -1):
                j = 1 - dx
                packs[(0, dz, j)] = [
                    copy(pq.at[sec, 0:4], rq.at[sec, 0, dz, j, 0:4], (dx, 0, dz)),
                    copy(ps.at[sec], rs.at[sec, 0, dz, j], (dx, 0, dz)),
                ]
                pack_relays[(dz, j)] = [
                    copy(rq.at[sec, 0, dz, j, 0:4], rq.at[sec, 1, dz, j, 0:4], (0, 1, 0)),
                    copy(rs.at[sec, 0, dz, j], rs.at[sec, 1, dz, j], (0, 1, 0)),
                ]

        for pair in x_copies:
            for c in pair:
                c.start()
        for c in y_copies:
            c.start()
        pack(sec, q, s)
        for both in packs.values():
            for c in both:
                c.start()

        for k in range(nx):
            for f in range(5):
                QF[f, HALO + k, own_y] = q[f, k].astype(F32)
            SA[HALO + k, own_y] = s[k]

        def windows(g, dy, fields):
            rows = far_y if dy else own_y
            for f in range(fields + 1):
                if f < fields:
                    own = pq[sec, f] if (g, dy) == (1, 0) else rq[sec, dy, 0, g, f]
                    own, far = own.astype(F32), rq[sec, dy, 1, g, f].astype(F32)
                    WQ[f, 2 * g, rows] = jnp.where(lower, far, own)
                    WQ[f, 2 * g + 1, rows] = jnp.where(lower, own, far)
                else:
                    own = ps[sec] if (g, dy) == (1, 0) else rs[sec, dy, 0, g]
                    far = rs[sec, dy, 1, g]
                    WA[2 * g, rows] = jnp.where(lower, far, own)
                    WA[2 * g + 1, rows] = jnp.where(lower, own, far)

        for c in y_copies:
            c.wait_recv()
        for k in range(nx):
            for f in range(5):
                QF[f, HALO + k, far_y] = yq[sec, f, k].astype(F32)
            SA[HALO + k, far_y] = ys[sec, k]
        for which in ((0, 1, 1), (1, 0, 1), (1, 1, 1)):
            for c in packs[which]:
                c.wait_recv()
        windows(1, 0, 5)
        windows(1, 1, 4)

        def line_flux(fields, d, axis):
            left, right = [], []
            for c in fields:
                l, r = edges(c, up(c, axis), down(c, axis), up(c, axis, 2), down(c, axis, 2))
                left.append(l)
                right.append(up(r, axis))
            return [v - down(v, axis) for v in face_flux(left, right, d)]

        lo = line_flux([WQ[f, 2, own_y] for f in range(5)], 2, 1)
        hi = line_flux([WQ[f, 3, own_y] for f in range(5)], 2, 1)
        for f in range(5):
            ZB[f] = jnp.where(lower, hi[f], lo[f])

        near = jnp.logical_or(lane < REACH, lane >= nz - REACH)

        def side_flux(k, carry):
            p = HALO + k
            ychange = line_flux([QF[f, p] for f in range(5)], 1, 0)
            zchange = line_flux([QF[f, p, own_y] for f in range(5)], 2, 1)
            shift = nz - half - slot * k
            for f in range(5):
                z = jnp.where(near, pltpu.roll(ZB[f], shift, 1), zchange[f])
                T[f, k] = ychange[f][own_y] + z
            return carry

        lax.fori_loop(0, nx, side_flux, 0)

        for side in (0, 1):
            for c in x_copies[side]:
                c.wait_recv()
            for c in relays[side]:
                c.start()
        for (dz, j), both in pack_relays.items():
            for c in packs[(0, dz, j)]:
                c.wait_recv()
            for c in both:
                c.start()
        for side in (0, 1):
            base = 0 if side == 0 else HALO + nx
            ebase = HALO - REACH if side == 0 else HALO + nx
            for k in range(HALO):
                for f in range(4):
                    QF[f, base + k, own_y] = xq[sec, side, f, k].astype(F32)
                SA[base + k, own_y] = xs[sec, side, k]
            for k in range(REACH):
                QF[4, ebase + k, own_y] = xe[sec, side, k].astype(F32)

        def x_face(p):
            left, right = [], []
            for f in range(5):
                v = [QF[f, p + o, own_y] for o in range(-2, 4)]
                left.append(edges(v[2], v[3], v[1], v[4], v[0])[0])
                right.append(edges(v[3], v[4], v[2], v[5], v[1])[1])
            return face_flux(left, right, 0)

        def x_flux(k, before):
            h = x_face(HALO + k)
            for f in range(5):
                T[f, k] = T[f, k] + (h[f] - before[f])
            return tuple(h)

        lax.fori_loop(0, nx, x_flux, tuple(x_face(HALO - 1)), unroll=2)

        windows(0, 0, 4)
        windows(2, 0, 4)
        for side in (0, 1):
            base = 0 if side == 0 else HALO + nx
            for c in relays[side]:
                c.wait_recv()
            for k in range(HALO):
                for f in range(4):
                    QF[f, base + k, far_y] = yxq[sec, side, f, k].astype(F32)
                SA[base + k, far_y] = yxs[sec, side, k]
        for both in pack_relays.values():
            for c in both:
                c.wait_recv()
        windows(0, 1, 4)
        windows(2, 1, 4)

        def velocities(p, carry):
            inv = 1.0 / QF[0, p]
            INV[p] = inv
            for a in range(3):
                U[a, p] = QF[1 + a, p] * inv
            return carry

        lax.fori_loop(0, px, velocities, 0, unroll=3)
        for n in range(6):
            inv = 1.0 / WQ[0, n]
            WI[n] = inv
            for a in range(3):
                WU[a, n] = WQ[1 + a, n] * inv

        def stencil_terms(g, c, around):
            div = g[0][0] + g[1][1] + g[2][2]
            total = div * div + g[0][0] * g[0][0] + g[1][1] * g[1][1] + g[2][2] * g[2][2]
            total = total + 2.0 * (g[0][1] * g[1][0] + g[0][2] * g[2][0] + g[1][2] * g[2][1])
            source = (alpha_reg * 0.25) * total
            w = [(alpha_reg * 0.5) * (c + n) for n in around]
            scale = 1.0 / (c + ((w[0] + w[1]) + (w[2] + w[3]) + (w[4] + w[5])))
            return [v * scale for v in w] + [source * scale]

        def coefficients(p, carry):
            g = []
            for a in range(3):
                u = U[a, p]
                g.append([
                    U[a, p + 1] - U[a, p - 1], up(u, 0) - down(u, 0), up(u, 1) - down(u, 1),
                ])
            c = INV[p]
            around = [INV[p + 1], INV[p - 1], up(c, 0), down(c, 0), up(c, 1), down(c, 1)]
            for n, v in enumerate(stencil_terms(g, c, around)):
                CO[n, p] = v
            return carry

        lax.fori_loop(1, px - 1, coefficients, 0, unroll=2)

        def in_x(ref, n):
            v = ref[n]
            after = ref[n + 2] if n < 4 else None
            before = ref[n - 2] if n > 1 else None
            return x_next(v, n, after), x_prev(v, n, before)

        for n in range(6):
            g = []
            for a in range(3):
                u = WU[a, n]
                hi_x, lo_x = in_x(WU.at[a], n)
                g.append([hi_x - lo_x, up(u, 0) - down(u, 0), up(u, 1) - down(u, 1)])
            c = WI[n]
            around = list(in_x(WI, n)) + [up(c, 0), down(c, 0), up(c, 1), down(c, 1)]
            for m, v in enumerate(stencil_terms(g, c, around)):
                WC[m, n] = v

        def jacobi(co, c, xp, xm):
            out = co(6) + co(0) * xp + co(1) * xm
            out = out + (co(2) * up(c, 0) + co(3) * down(c, 0))
            return out + (co(4) * up(c, 1) + co(5) * down(c, 1))

        read, write = SA, SB
        wread, wwrite = WA, WB
        for step in range(SWEEPS):
            def one(p, carry, read=read, write=write):
                write[p] = jacobi(lambda m: CO[m, p], read[p], read[p + 1], read[p - 1])
                return carry

            lax.fori_loop(step + 1, px - 1 - step, one, 0, unroll=2)
            for n in range(6):
                xp, xm = in_x(wread, n)
                wwrite[n] = jacobi(lambda m: WC[m, n], wread[n], xp, xm)
            read, write = write, read
            wread, wwrite = wwrite, wread
        S, WS = read, wread

        edge = jnp.logical_or(lane2 < SWEEPS, lane2 >= nz - SWEEPS)
        joined = [jnp.where(lower2, WS[2 * g + 1], WS[2 * g]) for g in range(3)]
        for k in range(-1, nx + 1):
            p = HALO + k
            g, at = (k + nx) // nx, (k + nx) % nx
            S[p] = jnp.where(edge, pltpu.roll(joined[g], nz - half - slot * at, 1), S[p])
        diffs = []
        for n in (2, 3):
            v = WS[n, own_y]
            e = v * WU[2, n, own_y]
            diffs.append((up(v, 1) - down(v, 1), up(e, 1) - down(e, 1)))
        for i in (0, 1):
            ZB[i] = jnp.where(lower, diffs[1][i], diffs[0][i])
        ends = jnp.logical_or(lane == 0, lane == nz - 1)

        def finish(k, carry):
            p = HALO + k
            shift = nz - half - slot * k
            push = [T[f, k] for f in range(5)]
            xp, xm = S[p + 1, own_y], S[p - 1, own_y]
            push[1] = push[1] + 0.5 * (xp - xm)
            power = xp * U[0, p + 1, own_y] - xm * U[0, p - 1, own_y]
            sy = S[p]
            push[2] = push[2] + 0.5 * (up(sy, 0) - down(sy, 0))[own_y]
            e = sy * U[1, p]
            power = power + (up(e, 0) - down(e, 0))[own_y]
            sz = S[p, own_y]
            dz = jnp.where(ends, pltpu.roll(ZB[0], shift, 1), up(sz, 1) - down(sz, 1))
            push[3] = push[3] + 0.5 * dz
            e = sz * U[2, p, own_y]
            power = power + jnp.where(ends, pltpu.roll(ZB[1], shift, 1), up(e, 1) - down(e, 1))
            push[4] = push[4] + 0.5 * power
            for f in range(5):
                initial = cons[f, k].astype(F32)
                moved = initial - time_step * push[f]
                new_out[f, k] = 0.5 * (moved + q[f, k].astype(F32))
                stq[sec + 1, f, k] = moved.astype(BF16)
            ent_out[k] = sz
            sts[sec + 1, k] = sz
            return carry

        lax.fori_loop(0, nx, finish, 0, unroll=2)
        for c in everything:
            c.wait_send()
        return carry

    stq[0] = cons[...]
    sts[0] = sigma[...]
    barrier = pltpu.get_barrier_semaphore()
    for peer in peers:
        pl.semaphore_signal(barrier, inc=1, device_id=dev(*peer), device_id_type=MESH)
    pl.semaphore_wait(barrier, len(peers))
    lax.fori_loop(0, 2, section, 0)


def slot_ok(nz, nx):
    return nz % nx == 0 and (nz // nx) & (nz // nx - 1) == 0


def solution(mesh):
    counts = (mesh.shape["gx"], mesh.shape["gy"], mesh.shape["gz"])
    assert counts[1] == 2 and counts[2] == 2

    def step(conserved, sigma_prev):
        _, nx, ny, nz = conserved.shape
        px = nx + 2 * HALO
        wide = (2 * ny, nz)
        assert nx >= HALO and nz // nx >= 4 * SWEEPS and slot_ok(nz, nx)
        vmem = pl.BlockSpec(memory_space=pltpu.VMEM)
        return pl.pallas_call(
            functools.partial(kernel, counts),
            out_shape=(
                jax.ShapeDtypeStruct((5, nx, ny, nz), F32),
                jax.ShapeDtypeStruct((nx, ny, nz), F32),
            ),
            in_specs=[vmem, vmem],
            out_specs=(vmem, vmem),
            scratch_shapes=[
                pltpu.VMEM((2, 2, 4, HALO, ny, nz), BF16),
                pltpu.VMEM((2, 2, REACH, ny, nz), BF16),
                pltpu.VMEM((2, 2, HALO, ny, nz), F32),
                pltpu.VMEM((2, 5, nx, ny, nz), BF16),
                pltpu.VMEM((2, nx, ny, nz), F32),
                pltpu.VMEM((2, 2, 4, HALO, ny, nz), BF16),
                pltpu.VMEM((2, 2, HALO, ny, nz), F32),
                pltpu.VMEM((2, 5, ny, nz), BF16),
                pltpu.VMEM((2, ny, nz), F32),
                pltpu.VMEM((2, 2, 2, 3, 5, ny, nz), BF16),
                pltpu.VMEM((2, 2, 2, 3, ny, nz), F32),
                pltpu.VMEM((3, 5, nx, ny, nz), BF16),
                pltpu.VMEM((3, nx, ny, nz), F32),
                pltpu.VMEM((5, px) + wide, F32),
                pltpu.VMEM((3, px) + wide, F32),
                pltpu.VMEM((px,) + wide, F32),
                pltpu.VMEM((7, px) + wide, F32),
                pltpu.VMEM((px,) + wide, F32),
                pltpu.VMEM((px,) + wide, F32),
                pltpu.VMEM((5, 6) + wide, F32),
                pltpu.VMEM((3, 6) + wide, F32),
                pltpu.VMEM((6,) + wide, F32),
                pltpu.VMEM((7, 6) + wide, F32),
                pltpu.VMEM((6,) + wide, F32),
                pltpu.VMEM((6,) + wide, F32),
                pltpu.VMEM((5, ny, nz), F32),
                pltpu.VMEM((5, nx, ny, nz), F32),
                pltpu.SemaphoreType.DMA((2, 34)),
                pltpu.SemaphoreType.DMA((2, 34)),
            ],
            compiler_params=pltpu.CompilerParams(collective_id=0, has_side_effects=True),
        )(conserved, sigma_prev)

    return jax.shard_map(
        step,
        mesh=mesh,
        in_specs=(P(None, "gx", "gy", "gz"), P("gx", "gy", "gz")),
        out_specs=(P(None, "gx", "gy", "gz"), P("gx", "gy", "gz")),
        check_vma=False,
    )
```

time: 35 us -> 34.3 us (0.980)
  Pallas kernels: 31.9 us -> 31.2 us
    pallas_call x1, Pallas kernels: 31.9 us -> 31.2 us  [step(): pl.pallas_call(functools.partial(kernel, counts), out_shape=(jax.ShapeDty...]
where the time goes in v2:
time: 34.3 us; the launch traced here: 34.1 us
  Pallas kernels  31.2 us (91%)
  local copies, waits for them, and re-layouts  2.22 us (6%)
  between operations  0.65 us (2%)
    pallas_call x1, Pallas kernels, step(): pl.pallas_call(functools.partial(kernel, counts), out_shape=(jax.ShapeDty...  31.2 us
    unnamed x4, local copies, waits for them, and re-layouts  2.22 us

profile of v2, /device:TPU:0, one launch (start us, length us, event | category | flops | bytes accessed | tf_op | source)
XLA Modules:
  0.0 34.1 jit_solution(2070585618819798663)
XLA Ops:
  0.6 31.2 %shard_map.41 = (f32[5,8,8,128]{3,2,1,0:T(8,128)}, f32[8,8,128]{2,1,0:T(8,128)}) custom-call(bf16[5,8,8,128]{3,2,1,0:T(8,128)(2,1)} %cons.1, f32[8,8,128]{2,1,0:T(8,128)} %sigma.1), custom_call_target="tpu_custom_call" | custom-call | tf_op jit(solution)/shard_map/pallas_call | solution.py:409
  31.9 0.0 copy-start
  31.9 1.6 %copy.6 = f32[5,8,8,128]{3,2,1,0:T(8,128)} copy(f32[5,8,8,128]{3,2,1,0:T(8,128)} %get-tuple-element.4) | data formatting | bytes 327680
  33.5 0.0 copy-done
  33.5 0.6 %copy.7 = f32[8,8,128]{2,1,0:T(8,128)} copy(f32[8,8,128]{2,1,0:T(8,128)S(1)} %copy-done) | data formatting | bytes 65536
Async XLA Ops:
  31.9 1.6 %copy-start = (f32[8,8,128]{2,1,0:T(8,128)S(1)}, f32[8,8,128]{2,1,0:T(8,128)}, u32[]{:S(2)}) copy-start(f32[8,8,128]{2,1,0:T(8,128)} %get-tuple-element.5) | copy-start | bytes 98308

commit v3 on v2

--- a/solution.py
+++ b/solution.py
@@ -208,7 +208,52 @@
                 T[f, k] = ychange[f][own_y] + z
             return carry
 
-        lax.fori_loop(0, nx, side_flux, 0)
+        lax.fori_loop(0, nx, side_flux, 0, unroll=2)
+
+        def velocities(p, carry):
+            inv = 1.0 / QF[0, p]
+            INV[p] = inv
+            for a in range(3):
+                U[a, p] = QF[1 + a, p] * inv
+            return carry
+
+        def stencil_terms(g, c, around):
+            div = g[0][0] + g[1][1] + g[2][2]
+            total = div * div + g[0][0] * g[0][0] + g[1][1] * g[1][1] + g[2][2] * g[2][2]
+            total = total + 2.0 * (g[0][1] * g[1][0] + g[0][2] * g[2][0] + g[1][2] * g[2][1])
+            source = (alpha_reg * 0.25) * total
+            w = [(alpha_reg * 0.5) * (c + n) for n in around]
+            scale = 1.0 / (c + ((w[0] + w[1]) + (w[2] + w[3]) + (w[4] + w[5])))
+            return [v * scale for v in w] + [source * scale]
+
+        def coefficients(p, carry):
+            g = []
+            for a in range(3):
+                u = U[a, p]
+                g.append([
+                    U[a, p + 1] - U[a, p - 1], up(u, 0) - down(u, 0), up(u, 1) - down(u, 1),
+                ])
+            c = INV[p]
+            around = [INV[p + 1], INV[p - 1], up(c, 0), down(c, 0), up(c, 1), down(c, 1)]
+            for n, v in enumerate(stencil_terms(g, c, around)):
+                CO[n, p] = v
+            return carry
+
+        def jacobi(co, c, xp, xm):
+            out = co(6) + co(0) * xp + co(1) * xm
+            out = out + (co(2) * up(c, 0) + co(3) * down(c, 0))
+            return out + (co(4) * up(c, 1) + co(5) * down(c, 1))
+
+        def main_sweep(step, planes):
+            read, write = (SA, SB) if step % 2 == 0 else (SB, SA)
+            for p in planes:
+                write[p] = jacobi(lambda m: CO[m, p], read[p], read[p + 1], read[p - 1])
+
+        inner = [range(HALO + 1 + t, HALO + nx - 1 - t) for t in range(SWEEPS)]
+        lax.fori_loop(HALO, HALO + nx, velocities, 0, unroll=4)
+        lax.fori_loop(inner[0].start, inner[0].stop, coefficients, 0, unroll=3)
+        for step in range(SWEEPS):
+            main_sweep(step, inner[step])
 
         for side in (0, 1):
             for c in x_copies[side]:
@@ -244,7 +289,7 @@
                 T[f, k] = T[f, k] + (h[f] - before[f])
             return tuple(h)
 
-        lax.fori_loop(0, nx, x_flux, tuple(x_face(HALO - 1)), unroll=2)
+        lax.fori_loop(0, nx, x_flux, tuple(x_face(HALO - 1)), unroll=4)
 
         windows(0, 0, 4)
         windows(2, 0, 4)
@@ -262,43 +307,18 @@
         windows(0, 1, 4)
         windows(2, 1, 4)
 
-        def velocities(p, carry):
-            inv = 1.0 / QF[0, p]
-            INV[p] = inv
-            for a in range(3):
-                U[a, p] = QF[1 + a, p] * inv
-            return carry
-
-        lax.fori_loop(0, px, velocities, 0, unroll=3)
+        for base in (0, HALO + nx):
+            for p in range(base, base + HALO):
+                velocities(p, 0)
         for n in range(6):
             inv = 1.0 / WQ[0, n]
             WI[n] = inv
             for a in range(3):
                 WU[a, n] = WQ[1 + a, n] * inv
 
-        def stencil_terms(g, c, around):
-            div = g[0][0] + g[1][1] + g[2][2]
-            total = div * div + g[0][0] * g[0][0] + g[1][1] * g[1][1] + g[2][2] * g[2][2]
-            total = total + 2.0 * (g[0][1] * g[1][0] + g[0][2] * g[2][0] + g[1][2] * g[2][1])
-            source = (alpha_reg * 0.25) * total
-            w = [(alpha_reg * 0.5) * (c + n) for n in around]
-            scale = 1.0 / (c + ((w[0] + w[1]) + (w[2] + w[3]) + (w[4] + w[5])))
-            return [v * scale for v in w] + [source * scale]
-
-        def coefficients(p, carry):
-            g = []
-            for a in range(3):
-                u = U[a, p]
-                g.append([
-                    U[a, p + 1] - U[a, p - 1], up(u, 0) - down(u, 0), up(u, 1) - down(u, 1),
-                ])
-            c = INV[p]
-            around = [INV[p + 1], INV[p - 1], up(c, 0), down(c, 0), up(c, 1), down(c, 1)]
-            for n, v in enumerate(stencil_terms(g, c, around)):
-                CO[n, p] = v
-            return carry
-
-        lax.fori_loop(1, px - 1, coefficients, 0, unroll=2)
+        for p in range(1, px - 1):
+            if p not in inner[0]:
+                coefficients(p, 0)
 
         def in_x(ref, n):
             v = ref[n]
@@ -317,25 +337,14 @@
             for m, v in enumerate(stencil_terms(g, c, around)):
                 WC[m, n] = v
 
-        def jacobi(co, c, xp, xm):
-            out = co(6) + co(0) * xp + co(1) * xm
-            out = out + (co(2) * up(c, 0) + co(3) * down(c, 0))
-            return out + (co(4) * up(c, 1) + co(5) * down(c, 1))
-
-        read, write = SA, SB
         wread, wwrite = WA, WB
         for step in range(SWEEPS):
-            def one(p, carry, read=read, write=write):
-                write[p] = jacobi(lambda m: CO[m, p], read[p], read[p + 1], read[p - 1])
-                return carry
-
-            lax.fori_loop(step + 1, px - 1 - step, one, 0, unroll=2)
+            main_sweep(step, [p for p in range(step + 1, px - 1 - step) if p not in inner[step]])
             for n in range(6):
                 xp, xm = in_x(wread, n)
                 wwrite[n] = jacobi(lambda m: WC[m, n], wread[n], xp, xm)
-            read, write = write, read
             wread, wwrite = wwrite, wread
-        S, WS = read, wread
+        S, WS = (SA if SWEEPS % 2 == 0 else SB), wread
 
         edge = jnp.logical_or(lane2 < SWEEPS, lane2 >= nz - SWEEPS)
         joined = [jnp.where(lower2, WS[2 * g + 1], WS[2 * g]) for g in range(3)]
@@ -378,7 +387,7 @@
             sts[sec + 1, k] = sz
             return carry
 
-        lax.fori_loop(0, nx, finish, 0, unroll=2)
+        lax.fori_loop(0, nx, finish, 0, unroll=4)
         for c in everything:
             c.wait_send()
         return carry
@@ -409,8 +418,8 @@
         return pl.pallas_call(
             functools.partial(kernel, counts),
             out_shape=(
-                jax.ShapeDtypeStruct((5, nx, ny, nz), F32),
-                jax.ShapeDtypeStruct((nx, ny, nz), F32),
+                pltpu.VMEM((5, nx, ny, nz), F32),
+                pltpu.VMEM((nx, ny, nz), F32),
             ),
             in_specs=[vmem, vmem],
             out_specs=(vmem, vmem),

time: 34.3 us -> 26.8 us (0.78)
  Pallas kernels: 31.2 us -> 24.7 us
  local copies, waits for them, and re-layouts: 2.22 us -> 1.28 us
    pallas_call x1, Pallas kernels: 31.2 us -> 24.7 us  [step(): pl.pallas_call(functools.partial(kernel, counts), out_shape=(pltpu.VMEM((...]
    unnamed x4 -> x2, local copies, waits for them, and re-layouts: 2.22 us -> 1.28 us
where the time goes in v3:
time: 26.8 us; the launch traced here: 26.6 us
  Pallas kernels  24.7 us (92%)
  local copies, waits for them, and re-layouts  1.28 us (5%)
  between operations  0.64 us (2%)
    pallas_call x1, Pallas kernels, step(): pl.pallas_call(functools.partial(kernel, counts), out_shape=(pltpu.VMEM((...  24.7 us
    unnamed x2, local copies, waits for them, and re-layouts  1.28 us

profile of v3, /device:TPU:0, one launch (start us, length us, event | category | flops | bytes accessed | tf_op | source)
XLA Modules:
  0.0 26.6 jit_solution(17976090916157982371)
XLA Ops:
  0.6 24.7 %shard_map.41 = (f32[5,8,8,128]{3,2,1,0:T(8,128)S(1)}, f32[8,8,128]{2,1,0:T(8,128)S(1)}) custom-call(bf16[5,8,8,128]{3,2,1,0:T(8,128)(2,1)} %cons.1, f32[8,8,128]{2,1,0:T(8,128)} %sigma.1), custom_call_target="tpu_custom_call" | custom-call | tf_op jit(solution)/shard_map/pallas_call | solution.py:418
  25.4 0.7 %copy.6 = f32[5,8,8,128]{3,2,1,0:T(8,128)} copy(f32[5,8,8,128]{3,2,1,0:T(8,128)S(1)} %get-tuple-element.2) | data formatting | bytes 327680
  26.0 0.6 %copy.7 = f32[8,8,128]{2,1,0:T(8,128)} copy(f32[8,8,128]{2,1,0:T(8,128)S(1)} %get-tuple-element.3) | data formatting | bytes 65536

commit v4 on v3

--- a/solution.py
+++ b/solution.py
@@ -51,7 +51,7 @@
 
 
 def kernel(counts, cons, sigma, new_out, ent_out, xq, xe, xs, yq, ys, yxq, yxs, pq, ps, rq, rs,
-           stq, sts, QF, U, INV, CO, SA, SB, WQ, WU, WI, WC, WA, WB, ZB, T, send_sem, recv_sem):
+           stq, sts, stb, QF, U, INV, CO, SA, SB, WQ, WU, WI, WC, WA, WB, ZB, T, send_sem, recv_sem):
     gx, gy, gz = lax.axis_index("gx"), lax.axis_index("gy"), lax.axis_index("gz")
     nx, ny, nz = sigma.shape
     px = nx + 2 * HALO
@@ -115,7 +115,7 @@
             b = nx - REACH if side == 0 else 0
             x_copies.append([
                 copy(q.at[0:4, a:a + HALO], xq.at[sec, side], to),
-                copy(s.at[a:a + HALO], xs.at[sec, side], to),
+                copy(stb.at[sec, a:a + HALO], xs.at[sec, side], to),
                 copy(q.at[4, b:b + REACH], xe.at[sec, side], to),
             ])
         y_copies = [copy(q, yq.at[sec], (0, 1, 0)), copy(s, ys.at[sec], (0, 1, 0))]
@@ -271,7 +271,7 @@
             for k in range(HALO):
                 for f in range(4):
                     QF[f, base + k, own_y] = xq[sec, side, f, k].astype(F32)
-                SA[base + k, own_y] = xs[sec, side, k]
+                SA[base + k, own_y] = xs[sec, side, k].astype(F32)
             for k in range(REACH):
                 QF[4, ebase + k, own_y] = xe[sec, side, k].astype(F32)
 
@@ -300,7 +300,7 @@
             for k in range(HALO):
                 for f in range(4):
                     QF[f, base + k, far_y] = yxq[sec, side, f, k].astype(F32)
-                SA[base + k, far_y] = yxs[sec, side, k]
+                SA[base + k, far_y] = yxs[sec, side, k].astype(F32)
         for both in pack_relays.values():
             for c in both:
                 c.wait_recv()
@@ -385,6 +385,7 @@
                 stq[sec + 1, f, k] = moved.astype(BF16)
             ent_out[k] = sz
             sts[sec + 1, k] = sz
+            stb[sec + 1, k] = sz.astype(BF16)
             return carry
 
         lax.fori_loop(0, nx, finish, 0, unroll=4)
@@ -394,6 +395,7 @@
 
     stq[0] = cons[...]
     sts[0] = sigma[...]
+    stb[0] = sigma[...].astype(BF16)
     barrier = pltpu.get_barrier_semaphore()
     for peer in peers:
         pl.semaphore_signal(barrier, inc=1, device_id=dev(*peer), device_id_type=MESH)
@@ -426,17 +428,18 @@
             scratch_shapes=[
                 pltpu.VMEM((2, 2, 4, HALO, ny, nz), BF16),
                 pltpu.VMEM((2, 2, REACH, ny, nz), BF16),
-                pltpu.VMEM((2, 2, HALO, ny, nz), F32),
+                pltpu.VMEM((2, 2, HALO, ny, nz), BF16),
                 pltpu.VMEM((2, 5, nx, ny, nz), BF16),
                 pltpu.VMEM((2, nx, ny, nz), F32),
                 pltpu.VMEM((2, 2, 4, HALO, ny, nz), BF16),
-                pltpu.VMEM((2, 2, HALO, ny, nz), F32),
+                pltpu.VMEM((2, 2, HALO, ny, nz), BF16),
                 pltpu.VMEM((2, 5, ny, nz), BF16),
                 pltpu.VMEM((2, ny, nz), F32),
                 pltpu.VMEM((2, 2, 2, 3, 5, ny, nz), BF16),
                 pltpu.VMEM((2, 2, 2, 3, ny, nz), F32),
                 pltpu.VMEM((3, 5, nx, ny, nz), BF16),
                 pltpu.VMEM((3, nx, ny, nz), F32),
+                pltpu.VMEM((3, nx, ny, nz), BF16),
                 pltpu.VMEM((5, px) + wide, F32),
                 pltpu.VMEM((3, px) + wide, F32),
                 pltpu.VMEM((px,) + wide, F32),

time: 26.8 us -> 26.5 us (0.989)
  Pallas kernels: 24.7 us -> 24.4 us
    pallas_call x1, Pallas kernels: 24.7 us -> 24.4 us  [step(): pl.pallas_call(functools.partial(kernel, counts), out_shape=(pltpu.VMEM((...]
where the time goes in v4:
time: 26.5 us; the launch traced here: 26.3 us
  Pallas kernels  24.4 us (92%)
  local copies, waits for them, and re-layouts  1.28 us (5%)
  between operations  0.64 us (2%)
    pallas_call x1, Pallas kernels, step(): pl.pallas_call(functools.partial(kernel, counts), out_shape=(pltpu.VMEM((...  24.4 us
    unnamed x2, local copies, waits for them, and re-layouts  1.28 us

profile of v4, /device:TPU:0, one launch (start us, length us, event | category | flops | bytes accessed | tf_op | source)
XLA Modules:
  0.0 26.3 jit_solution(346391122610077691)
XLA Ops:
  0.6 24.4 %shard_map.41 = (f32[5,8,8,128]{3,2,1,0:T(8,128)S(1)}, f32[8,8,128]{2,1,0:T(8,128)S(1)}) custom-call(bf16[5,8,8,128]{3,2,1,0:T(8,128)(2,1)} %cons.1, f32[8,8,128]{2,1,0:T(8,128)} %sigma.1), custom_call_target="tpu_custom_call" | custom-call | tf_op jit(solution)/shard_map/pallas_call | solution.py:420
  25.0 0.7 %copy.6 = f32[5,8,8,128]{3,2,1,0:T(8,128)} copy(f32[5,8,8,128]{3,2,1,0:T(8,128)S(1)} %get-tuple-element.2) | data formatting | bytes 327680
  25.7 0.6 %copy.7 = f32[8,8,128]{2,1,0:T(8,128)} copy(f32[8,8,128]{2,1,0:T(8,128)S(1)} %get-tuple-element.3) | data formatting | bytes 65536

commit v5 on v4

--- a/solution.py
+++ b/solution.py
@@ -208,7 +208,7 @@
                 T[f, k] = ychange[f][own_y] + z
             return carry
 
-        lax.fori_loop(0, nx, side_flux, 0, unroll=2)
+        lax.fori_loop(0, nx, side_flux, 0, unroll=4)
 
         def velocities(p, carry):
             inv = 1.0 / QF[0, p]
@@ -388,7 +388,7 @@
             stb[sec + 1, k] = sz.astype(BF16)
             return carry
 
-        lax.fori_loop(0, nx, finish, 0, unroll=4)
+        lax.fori_loop(0, nx, finish, 0, unroll=nx)
         for c in everything:
             c.wait_send()
         return carry

time: 26.5 us -> 26.1 us (0.985)
  Pallas kernels: 24.4 us -> 24 us
    pallas_call x1, Pallas kernels: 24.4 us -> 24 us  [step(): pl.pallas_call(functools.partial(kernel, counts), out_shape=(pltpu.VMEM((...]
where the time goes in v5:
time: 26.1 us; the launch traced here: 26 us
  Pallas kernels  24 us (92%)
  local copies, waits for them, and re-layouts  1.28 us (5%)
  between operations  0.64 us (2%)
    pallas_call x1, Pallas kernels, step(): pl.pallas_call(functools.partial(kernel, counts), out_shape=(pltpu.VMEM((...  24 us
    unnamed x2, local copies, waits for them, and re-layouts  1.28 us

profile of v5, /device:TPU:0, one launch (start us, length us, event | category | flops | bytes accessed | tf_op | source)
XLA Modules:
  0.0 26.0 jit_solution(399229390313887016)
XLA Ops:
  0.6 24.0 %shard_map.41 = (f32[5,8,8,128]{3,2,1,0:T(8,128)S(1)}, f32[8,8,128]{2,1,0:T(8,128)S(1)}) custom-call(bf16[5,8,8,128]{3,2,1,0:T(8,128)(2,1)} %cons.1, f32[8,8,128]{2,1,0:T(8,128)} %sigma.1), custom_call_target="tpu_custom_call" | custom-call | tf_op jit(solution)/shard_map/pallas_call | solution.py:420
  24.7 0.7 %copy.6 = f32[5,8,8,128]{3,2,1,0:T(8,128)} copy(f32[5,8,8,128]{3,2,1,0:T(8,128)S(1)} %get-tuple-element.2) | data formatting | bytes 327680
  25.3 0.6 %copy.7 = f32[8,8,128]{2,1,0:T(8,128)} copy(f32[8,8,128]{2,1,0:T(8,128)S(1)} %get-tuple-element.3) | data formatting | bytes 65536
